TPU v7x, 256 devices: a whole 4x4x8 slice. The times are simulated.
256 devices in a mesh: seq: 16 (over z, core), head: 8 (over x_lo, y), batch: 2 (over x_hi).
Axes of the slice: x: 4 (x_hi: 2, x_lo: 2; x = x_hi * 2 + x_lo), y: 4, z: 8, core: 2. Of those that a mesh axis runs over, the one named last changes fastest.
Arguments:
- queries: bfloat16 [8192, 4096], P(('batch', 'seq'), 'head'), parts along dimension 0, may hold values from -16 to 16, as said below
- key_rows: bfloat16 [8192, 1024], P(('batch', 'seq'), 'head'), parts along dimension 0, may hold values from -16 to 16
- value_rows: bfloat16 [8192, 1024], P(('batch', 'seq'), 'head'), parts along dimension 0, may hold values from -6 to 6
- out_grad: bfloat16 [8192, 4096], P(('batch', 'seq'), 'head'), parts along dimension 0, may hold values from -6 to 6
- tile_ids: int32 [64], P('batch'), parts along dimension 0, may hold values from 0 to 31, each once
- tile_mask: int32 [64, 32], P('batch'), parts along dimension 0, may hold values from 0 to 1, as said below
Outputs:
- attended: bfloat16 [8192, 4096], P(('batch', 'seq'), 'head'), parts along dimension 0
- query_grad: float32 [8192, 4096], P(('batch', 'seq'), 'head'), parts along dimension 0
- key_grad: float32 [8192, 1024], P(('batch', 'seq'), 'head'), parts along dimension 0
- value_grad: float32 [8192, 1024], P(('batch', 'seq'), 'head'), parts along dimension 0
There are 2 independent parts, one for each index of `batch`. A program takes and returns all parts, laid end to end along the dimension named above; each array names one. Nothing has to cross between parts.
Inputs may be any that keep to these rules, and one draw needn't show every extreme that they name: `queries`: in the hidden draw a few query rows equal scaled key rows of the same tile. `tile_mask`: 1 only where the key tile's index is at most the query tile's; 1 on the diagonal.
All inputs are finite; a program needn't handle non-finite values.
Results may differ from a plain program's by a relative error of at most 0.03.
Values may be sent and summed in bfloat16 or wider, within the bound.
A program may use at most 64 MiB of HBM per device.

v0:
```python
import math
import jax
import jax.numpy as jnp
from jax import lax
from jax.sharding import PartitionSpec as P

HD = 128
TILE = 128
far_below = -1e30


def tile_allowed(tile_mask, query_tiles, key_tiles):
    table = jnp.take(jnp.take(tile_mask, query_tiles, axis=0), key_tiles, axis=1) == 1
    same_tile = query_tiles[:, None] == key_tiles[None, :]
    inside = lax.broadcasted_iota(jnp.int32, (TILE, TILE), 0) >= lax.broadcasted_iota(
        jnp.int32, (TILE, TILE), 1
    )
    full = table[:, None, :, None] & (
        jnp.logical_not(same_tile)[:, None, :, None] | inside[None, :, None, :]
    )
    return full.reshape(query_tiles.shape[0] * TILE, key_tiles.shape[0] * TILE)


def sub_blocks(row_total, limit):
    block_rows = math.gcd(row_total, limit)
    return (block_rows, row_total // block_rows)


def per_device(queries, key_rows, value_rows, out_grad, tile_ids, tile_mask):
    row_count = queries.shape[0]
    group_count = key_rows.shape[1] // HD
    head_count = queries.shape[1] // (group_count * HD)
    factor = HD ** (-0.5)
    my_rank = lax.axis_index("seq")
    limit = 1024
    query_heads = queries.reshape(row_count, group_count, head_count, HD)
    grad_heads = out_grad.reshape(row_count, group_count, head_count, HD)
    query_tiles = lax.dynamic_slice_in_dim(
        tile_ids, my_rank * (row_count // TILE), row_count // TILE
    )

    def block_mask(first_row, row_total):
        key_tiles = lax.dynamic_slice_in_dim(tile_ids, first_row // TILE, row_total // TILE)
        return tile_allowed(tile_mask, query_tiles, key_tiles)

    def masked_scores(key_block, allowed):
        scores = (
            jnp.einsum("qghd,kgd->ghqk", query_heads, key_block, preferred_element_type=jnp.float32)
            * factor
        )
        return jnp.where(allowed[None, None], scores, far_below)

    def forward_block(carried, key_block, value_block, first_row):
        allowed = block_mask(first_row, key_block.shape[0])
        row_max, denominator, weighted = carried
        scores = masked_scores(key_block, allowed)
        new_max = jnp.maximum(row_max, jnp.max(scores, axis=-1))
        shrink = jnp.exp(row_max - new_max)
        softmax_terms = jnp.where(allowed[None, None], jnp.exp(scores - new_max[..., None]), 0.0)
        denominator = denominator * shrink + jnp.sum(softmax_terms, axis=-1)
        weighted = weighted * shrink[..., None] + jnp.einsum(
            "ghqk,kgd->ghqd",
            softmax_terms.astype(jnp.bfloat16),
            value_block,
            preferred_element_type=jnp.float32,
        )
        return (new_max, denominator, weighted)

    stat_shape = (group_count, head_count, row_count)
    initial = (
        jnp.full(stat_shape, far_below, jnp.float32),
        jnp.zeros(stat_shape, jnp.float32),
        jnp.zeros(stat_shape + (HD,), jnp.float32),
    )
    key_piece = lax.all_gather(key_rows, "seq", axis=0, tiled=True)
    value_piece = lax.all_gather(value_rows, "seq", axis=0, tiled=True)
    block_rows, number = sub_blocks(key_piece.shape[0], limit)

    def forward_advance(position, current):
        key_block = lax.dynamic_slice_in_dim(key_piece, position * block_rows, block_rows).reshape(
            block_rows, group_count, HD
        )
        value_block = lax.dynamic_slice_in_dim(
            value_piece, position * block_rows, block_rows
        ).reshape(block_rows, group_count, HD)
        return forward_block(current, key_block, value_block, position * block_rows)

    row_max, denominator, weighted = lax.fori_loop(0, number, forward_advance, initial)
    attended_heads = jnp.transpose(weighted / denominator[..., None], (2, 0, 1, 3))
    attended = attended_heads.reshape(row_count, group_count * head_count * HD).astype(jnp.bfloat16)
    log_total = row_max + jnp.log(denominator)
    row_delta = jnp.transpose(
        jnp.sum(
            grad_heads.astype(jnp.float32)
            * attended.reshape(row_count, group_count, head_count, HD).astype(jnp.float32),
            axis=-1,
        ),
        (1, 2, 0),
    )

    def backward_block(key_block, value_block, first_row):
        allowed = block_mask(first_row, key_block.shape[0])
        scores = masked_scores(key_block, allowed)
        softmax_terms = jnp.where(allowed[None, None], jnp.exp(scores - log_total[..., None]), 0.0)
        dprobs = jnp.einsum(
            "qghd,kgd->ghqk", grad_heads, value_block, preferred_element_type=jnp.float32
        )
        dscores = (softmax_terms * (dprobs - row_delta[..., None])).astype(jnp.bfloat16)
        query_part = (
            jnp.einsum("ghqk,kgd->qghd", dscores, key_block, preferred_element_type=jnp.float32)
            * factor
        )
        key_part = (
            jnp.einsum("ghqk,qghd->kgd", dscores, query_heads, preferred_element_type=jnp.float32)
            * factor
        )
        value_part = jnp.einsum(
            "ghqk,qghd->kgd",
            softmax_terms.astype(jnp.bfloat16),
            grad_heads,
            preferred_element_type=jnp.float32,
        )
        key_flat = key_part.reshape(key_block.shape[0], group_count * HD)
        value_flat = value_part.reshape(key_block.shape[0], group_count * HD)
        return (query_part, jnp.concatenate([key_flat, value_flat], axis=-1))

    gathered_keys, gathered_values = (
        lax.all_gather(key_rows, "seq", axis=0, tiled=True),
        lax.all_gather(value_rows, "seq", axis=0, tiled=True),
    )
    sweep_block_rows, number = sub_blocks(gathered_keys.shape[0], limit)

    def sweep_advance(query_sum, position):
        key_block = lax.dynamic_slice_in_dim(
            gathered_keys, position * sweep_block_rows, sweep_block_rows
        ).reshape(sweep_block_rows, group_count, HD)
        value_block = lax.dynamic_slice_in_dim(
            gathered_values, position * sweep_block_rows, sweep_block_rows
        ).reshape(sweep_block_rows, group_count, HD)
        query_part, key_value = backward_block(
            key_block, value_block, 0 + position * sweep_block_rows
        )
        return (query_sum + query_part, key_value)

    query_sum, stacked = lax.scan(
        sweep_advance,
        jnp.zeros((row_count, group_count, head_count, HD), jnp.float32),
        jnp.arange(number, dtype=jnp.int32),
    )
    query_sum, key_terms = (
        query_sum,
        stacked.reshape(gathered_keys.shape[0], 2 * group_count * HD),
    )
    own_terms = lax.psum_scatter(
        key_terms.astype(jnp.bfloat16), "seq", scatter_dimension=0, tiled=True
    ).astype(jnp.float32)
    query_grad = query_sum.reshape(row_count, group_count * head_count * HD)
    width = group_count * HD
    return (attended, query_grad, own_terms[:, :width], own_terms[:, width:])


def solution(mesh):
    return jax.shard_map(
        per_device,
        mesh=mesh,
        in_specs=(
            P(("batch", "seq"), "head"),
            P(("batch", "seq"), "head"),
            P(("batch", "seq"), "head"),
            P(("batch", "seq"), "head"),
            P("batch"),
            P("batch", None),
        ),
        out_specs=(
            P(("batch", "seq"), "head"),
            P(("batch", "seq"), "head"),
            P(("batch", "seq"), "head"),
            P(("batch", "seq"), "head"),
        ),
        check_vma=False,
    )
```

profile of v0, /device:TPU:2, one launch (start us, length us, event | category | flops | bytes accessed | tf_op | source)
XLA Modules:
  0.0 242.3 jit_solution(15315642816570585273)
XLA Ops:
  11.5 1.1 copy.42
  12.6 38.7 %all-gather.3.cloned.1.call-done = bf16[4096,128]{1,0:T(8,128)(2,1)} async-done(((bf16[256,128]{1,0:T(8,128)(2,1)}), bf16[4096,128]{1,0:T(8,128)(2,1)}) %all-gather.3.cloned.1.call-update) | async-done | bytes 1048592 | tf_op jit(solution)/shard_map/all_gather | solution.py:75
  51.4 39.0 %all-gather.5.cloned.1.call-done = bf16[4096,128]{1,0:T(8,128)(2,1)} async-done(((bf16[256,128]{1,0:T(8,128)(2,1)}), bf16[4096,128]{1,0:T(8,128)(2,1)}) %all-gather.5.cloned.1.call-update) | async-done | bytes 1048592 | tf_op jit(solution)/shard_map/all_gather | solution.py:76
  90.3 30.9 %while.35 = (s32[]{:T(128)}, f32[1,4,256]{2,1,0:T(4,128)S(1)}, f32[1,4,256]{2,1,0:T(4,128)S(1)}, f32[1,4,256,128]{3,2,1,0:T(8,128)S(1)}, s32[32]{0:T(128)}, /*in...) while((s32[]{:T(128)}, f32[1,4,256]{2,1,0:T(4,128)S(1)}, ...), condition=%wide.region_3.6_spmd.clone, body=%wide.region_0.5_spmd.clone.sunk | while | flops 551443584 | bytes 16618426 | solution.py:88
  92.7 1.8 fusion.100
  95.5 2.4 %fusion.103 = f32[1,4,256,128]{3,2,1,0:T(8,128)S(1)} fusion(f32[1024,256,4]{1,0,2:T(8,128)S(1)} %get-tuple-element.745, f32[4,256]{1,0:T(4,128)S(1)} %bitcast.245, pred[256,1024]{0,1:T(8,128)(4,1)S(1)} %copy.70, f32[1,4,256,128]{3,2,1,0:T(8,128)S(1)} %get-tuple-element.783, bf16[4096,128]{1,0:T(8,128)(2,1)} %get-tuple-element.807, ...), kind=kOutput, calls=%fused_computation.12.clone.1 | convolution fusion | flops 274071552 | bytes 5775365 | tf_op jit(solution)/shard_map/while/body/eval_jaxpr/ghqk,kgd->ghqd/dot_general | solution.py:61
  100.4 1.8 fusion.100
  103.3 2.4 %fusion.103 = f32[1,4,256,128]{3,2,1,0:T(8,128)S(1)} fusion(f32[1024,256,4]{1,0,2:T(8,128)S(1)} %get-tuple-element.745, f32[4,256]{1,0:T(4,128)S(1)} %bitcast.245, pred[256,1024]{0,1:T(8,128)(4,1)S(1)} %copy.70, f32[1,4,256,128]{3,2,1,0:T(8,128)S(1)} %get-tuple-element.783, bf16[4096,128]{1,0:T(8,128)(2,1)} %get-tuple-element.807, ...), kind=kOutput, calls=%fused_computation.12.clone.1 | convolution fusion | flops 274071552 | bytes 5775365 | tf_op jit(solution)/shard_map/while/body/eval_jaxpr/ghqk,kgd->ghqd/dot_general | solution.py:61
  108.2 1.8 fusion.100
  111.0 2.4 %fusion.103 = f32[1,4,256,128]{3,2,1,0:T(8,128)S(1)} fusion(f32[1024,256,4]{1,0,2:T(8,128)S(1)} %get-tuple-element.745, f32[4,256]{1,0:T(4,128)S(1)} %bitcast.245, pred[256,1024]{0,1:T(8,128)(4,1)S(1)} %copy.70, f32[1,4,256,128]{3,2,1,0:T(8,128)S(1)} %get-tuple-element.783, bf16[4096,128]{1,0:T(8,128)(2,1)} %get-tuple-element.807, ...), kind=kOutput, calls=%fused_computation.12.clone.1 | convolution fusion | flops 274071552 | bytes 5775365 | tf_op jit(solution)/shard_map/while/body/eval_jaxpr/ghqk,kgd->ghqd/dot_general | solution.py:61
  115.9 1.8 fusion.100
  118.8 2.4 %fusion.103 = f32[1,4,256,128]{3,2,1,0:T(8,128)S(1)} fusion(f32[1024,256,4]{1,0,2:T(8,128)S(1)} %get-tuple-element.745, f32[4,256]{1,0:T(4,128)S(1)} %bitcast.245, pred[256,1024]{0,1:T(8,128)(4,1)S(1)} %copy.70, f32[1,4,256,128]{3,2,1,0:T(8,128)S(1)} %get-tuple-element.783, bf16[4096,128]{1,0:T(8,128)(2,1)} %get-tuple-element.807, ...), kind=kOutput, calls=%fused_computation.12.clone.1 | convolution fusion | flops 274071552 | bytes 5775365 | tf_op jit(solution)/shard_map/while/body/eval_jaxpr/ghqk,kgd->ghqd/dot_general | solution.py:61
  121.6 49.8 %while.36 = (s32[]{:T(128)}, f32[256,1,4,128]{0,3,2,1:T(8,128)S(1)}, bf16[4,1024,256]{1,2,0:T(8,128)(2,1)}, s32[4]{0:T(128)S(1)}, bf16[4096,128]{1,0:T(8,128)(2,...) while((s32[]{:T(128)}, ...), condition=%wide.region_6.9_spmd.clone, body=%wide.region_5.8_spmd.clone.sunk | while | flops 1357005952 | bytes 25215972 | solution.py:145
  125.3 1.6 fusion.114
  126.9 1.5 fusion.117
  128.4 2.5 %fusion.115 = bf16[1,4,256,1024]{2,3,1,0:T(8,128)(2,1)S(1)} fusion(f32[1024,256,4]{1,0,2:T(8,128)S(1)} %fusion.114, f32[4,256]{1,0:T(4,128)S(1)} %bitcast.251, f32[4,256]{1,0:T(4,128)S(1)} %bitcast.253, pred[256,1024]{0,1:T(8,128)(4,1)S(1)} %copy.73, bf16[256,1,4,128]{0,3,2,1:T(8,128)(2,1)S(1)} %get-tuple-element.869, ...), kind=kOutput, calls=%fused_computation.40.clone.1 | convolution fusion | flops 275775488 | bytes 7086084 | tf_op jit(solution)/shard_map/while/body/eval_jaxpr/qghd,kgd->ghqk/dot_general | solution.py:105
  131.7 1.5 fusion.116
  137.7 1.6 fusion.114
  139.4 1.5 fusion.117
  140.9 2.5 %fusion.115 = bf16[1,4,256,1024]{2,3,1,0:T(8,128)(2,1)S(1)} fusion(f32[1024,256,4]{1,0,2:T(8,128)S(1)} %fusion.114, f32[4,256]{1,0:T(4,128)S(1)} %bitcast.251, f32[4,256]{1,0:T(4,128)S(1)} %bitcast.253, pred[256,1024]{0,1:T(8,128)(4,1)S(1)} %copy.73, bf16[256,1,4,128]{0,3,2,1:T(8,128)(2,1)S(1)} %get-tuple-element.869, ...), kind=kOutput, calls=%fused_computation.40.clone.1 | convolution fusion | flops 275775488 | bytes 7086084 | tf_op jit(solution)/shard_map/while/body/eval_jaxpr/qghd,kgd->ghqk/dot_general | solution.py:105
  144.2 1.5 fusion.116
  150.2 1.6 fusion.114
  151.8 1.5 fusion.117
  153.4 2.5 %fusion.115 = bf16[1,4,256,1024]{2,3,1,0:T(8,128)(2,1)S(1)} fusion(f32[1024,256,4]{1,0,2:T(8,128)S(1)} %fusion.114, f32[4,256]{1,0:T(4,128)S(1)} %bitcast.251, f32[4,256]{1,0:T(4,128)S(1)} %bitcast.253, pred[256,1024]{0,1:T(8,128)(4,1)S(1)} %copy.73, bf16[256,1,4,128]{0,3,2,1:T(8,128)(2,1)S(1)} %get-tuple-element.869, ...), kind=kOutput, calls=%fused_computation.40.clone.1 | convolution fusion | flops 275775488 | bytes 7086084 | tf_op jit(solution)/shard_map/while/body/eval_jaxpr/qghd,kgd->ghqk/dot_general | solution.py:105
  156.6 1.5 fusion.116
  162.6 1.6 fusion.114
  164.3 1.5 fusion.117
  165.8 2.5 %fusion.115 = bf16[1,4,256,1024]{2,3,1,0:T(8,128)(2,1)S(1)} fusion(f32[1024,256,4]{1,0,2:T(8,128)S(1)} %fusion.114, f32[4,256]{1,0:T(4,128)S(1)} %bitcast.251, f32[4,256]{1,0:T(4,128)S(1)} %bitcast.253, pred[256,1024]{0,1:T(8,128)(4,1)S(1)} %copy.73, bf16[256,1,4,128]{0,3,2,1:T(8,128)(2,1)S(1)} %get-tuple-element.869, ...), kind=kOutput, calls=%fused_computation.40.clone.1 | convolution fusion | flops 275775488 | bytes 7086084 | tf_op jit(solution)/shard_map/while/body/eval_jaxpr/qghd,kgd->ghqk/dot_general | solution.py:105
  169.1 1.5 fusion.116
  171.4 3.9 %copy.45 = bf16[4,1024,256]{2,1,0:T(8,128)(2,1)} copy(bf16[4,1024,256]{1,2,0:T(8,128)(2,1)} %get-tuple-element.424) | data formatting | bytes 4194304 | tf_op jit(solution)/shard_map/convert_element_type | solution.py:155
  177.2 57.0 %reduce-scatter.2.cloned.1.call-done = bf16[256,256]{1,0:T(8,128)(2,1)} async-done(((bf16[4096,256]{1,0:T(8,128)(2,1)}), bf16[256,256]{1,0:T(8,128)(2,1)}) %reduce-scatter.2.cloned.1.call-update) | async-done | bytes 131088 | tf_op jit(solution)/shard_map/reduce_scatter | solution.py:154
  234.2 1.6 fusion.75
  (143 shorter events, 38.6 us)
Async XLA Ops:
  7.2 2.4 copy-start
  7.2 44.2 %all-gather.3.cloned.1.call-start = ((), (), s32[]{:S(2)}) async-start(), calls=%async_computation.1 | async-start | bytes 1114112 | tf_op jit(solution)/shard_map/all_gather | solution.py:75
  7.9 82.4 %all-gather.5.cloned.1.call-start = ((), (), s32[]{:S(2)}) async-start(), calls=%async_computation.2 | async-start | bytes 1114112 | tf_op jit(solution)/shard_map/all_gather | solution.py:76
  8.7 225.6 %reduce-scatter.2.cloned.1.call-start = ((), (), s32[]{:S(2)}) async-start(), calls=%async_computation.3 | async-start | bytes 2228224 | tf_op jit(solution)/shard_map/reduce_scatter | solution.py:154
Sparse Core Ops, SparseCore 0:
  9.8 41.4 all-gather.2
  53.2 37.0 all-gather.4
  175.5 58.6 reduce-scatter.1
where the time goes:
time: 243 us; the launch traced here: 242 us
  waiting for transfers between devices  136 us (56%)
  matrix products  48.5 us (20%)
  local copies, waits for them, and re-layouts  22.7 us (9%)
  other arithmetic  17.7 us (7%)
  between operations  13.9 us (6%)
  loops' own time  3.33 us (1%)
    reduce_scatter x1, waiting for transfers between devices, per_device(): lax.psum_scatter(key_terms.astype(jnp.bfloat16), 'seq', scatter_dimension...  57 us
    all_gather x1, waiting for transfers between devices, per_device(): value_piece = lax.all_gather(value_rows, 'seq', axis=0, tiled=True)  39 us
    all_gather x1, waiting for transfers between devices, per_device(): key_piece = lax.all_gather(key_rows, 'seq', axis=0, tiled=True)  38.7 us
    dot_general x8, matrix products, masked_scores(): jnp.einsum('qghd,kgd->ghqk', query_heads, key_block, preferred_element_ty...  13.6 us
    dot_general x4, matrix products, backward_block(): jnp.einsum('qghd,kgd->ghqk', grad_heads, value_block, preferred_element_t...  9.81 us
    dot_general x4, matrix products, forward_block(): jnp.einsum('ghqk,kgd->ghqd', softmax_terms.astype(jnp.bfloat16), value_bl...  9.75 us
    dot_general x4, matrix products, backward_block(): jnp.einsum('ghqk,qghd->kgd', softmax_terms.astype(jnp.bfloat16), grad_hea...  6.03 us
    dot_general x4, matrix products, backward_block(): jnp.einsum('ghqk,kgd->qghd', dscores, key_block, preferred_element_type=j...  6.02 us
  transfers between devices with their start and end apart: 3, of which 3 were waited for; matrix products, arithmetic and copies ran while one was open for 2% of the time, Pallas kernels for 0%

commit v1 on v0

--- a/solution.py
+++ b/solution.py
@@ -7,6 +7,11 @@
 HD = 128
 TILE = 128
 far_below = -1e30
+
+
+def all_by_exchange(block, axis, along):
+    stack = jnp.stack([block] * lax.axis_size(axis))
+    return jnp.concatenate(lax.all_to_all(stack, axis, 0, 0), axis=along)
 
 
 def tile_allowed(tile_mask, query_tiles, key_tiles):
@@ -72,7 +77,7 @@
         jnp.zeros(stat_shape, jnp.float32),
         jnp.zeros(stat_shape + (HD,), jnp.float32),
     )
-    key_piece = lax.all_gather(key_rows, "seq", axis=0, tiled=True)
+    key_piece = all_by_exchange(key_rows, "seq", 0)
     value_piece = lax.all_gather(value_rows, "seq", axis=0, tiled=True)
     block_rows, number = sub_blocks(key_piece.shape[0], limit)
 

time: 243 us -> 215 us (0.88)
  waiting for transfers between devices: 136 us -> 108 us
  starting transfers between devices: 0.11 us -> 8.69 us
  other arithmetic: 17.7 us -> 12.5 us
  matrix products: 48.5 us -> 44.8 us
    all_gather x1, waiting for transfers between devices: 38.7 us -> 15.1 us  [per_device(): lax.all_gather(key_rows, 'seq', axis=0, tiled=True)]
    all_to_all x0 -> x1, starting transfers between devices: none -> 8.57 us  [all_by_exchange(): return jnp.concatenate(lax.all_to_all(stack, axis, 0, 0), axis=along)]
    and x8, other arithmetic: 5.9 us -> 0.65 us  [tile_allowed(): jnp.take(jnp.take(tile_mask, query_tiles, axis=0), key_tiles, axis=1) == 1]
    all_gather x1, waiting for transfers between devices: 39 us -> 34.1 us  [per_device(): value_piece = lax.all_gather(value_rows, 'seq', axis=0, tiled=True)]
    dot_general x8, matrix products: 13.6 us -> 9.85 us  [masked_scores(): jnp.einsum('qghd,kgd->ghqk', query_heads, key_block, preferred_element_ty...]
  transfers between devices with their start and end apart: 3 -> 4, of which waited for: 3 -> 3; matrix products, arithmetic and copies ran while one was open for 2% -> 15% of each run, Pallas kernels for 0% -> 0%
where the time goes in v1:
time: 215 us
  waiting for transfers between devices  108 us (50%)
  matrix products  44.8 us (21%)
  local copies, waits for them, and re-layouts  23.8 us (11%)
  between operations  13.9 us (6%)
  other arithmetic  12.5 us (6%)
  starting transfers between devices  8.69 us (4%)
  loops' own time  3.31 us (2%)
    reduce_scatter x1, waiting for transfers between devices, per_device(): lax.psum_scatter(key_terms.astype(jnp.bfloat16), 'seq', scatter_dimension...  57 us
    all_gather x1, waiting for transfers between devices, per_device(): value_piece = lax.all_gather(value_rows, 'seq', axis=0, tiled=True)  34.1 us
    all_gather x1, waiting for transfers between devices, per_device(): lax.all_gather(key_rows, 'seq', axis=0, tiled=True)  15.1 us
    dot_general x8, matrix products, masked_scores(): jnp.einsum('qghd,kgd->ghqk', query_heads, key_block, preferred_element_ty...  9.85 us
    dot_general x4, matrix products, backward_block(): jnp.einsum('qghd,kgd->ghqk', grad_heads, value_block, preferred_element_t...  9.84 us
    dot_general x4, matrix products, forward_block(): jnp.einsum('ghqk,kgd->ghqd', softmax_terms.astype(jnp.bfloat16), value_bl...  9.74 us
    all_to_all x1, starting transfers between devices, all_by_exchange(): return jnp.concatenate(lax.all_to_all(stack, axis, 0, 0), axis=along)  8.57 us
    dot_general x4, matrix products, backward_block(): jnp.einsum('ghqk,qghd->kgd', softmax_terms.astype(jnp.bfloat16), grad_hea...  6.15 us
  transfers between devices with their start and end apart: 4, of which 3 were waited for; matrix products, arithmetic and copies ran while one was open for 15% of the time, Pallas kernels for 0%

profile of v1, /device:TPU:2, one launch (start us, length us, event | category | flops | bytes accessed | tf_op | source)
XLA Modules:
  0.0 214.5 jit_solution(3538466680637001799)
XLA Ops:
  7.9 2.0 stack.2
  10.0 8.6 %all-to-all-start = ((bf16[16,256,128]{2,1,0:T(8,128)(2,1)}), bf16[16,256,128]{2,1,0:T(8,128)(2,1)S(1)}, u32[]{:S(2)}, u32[]{:S(2)}) async-start(bf16[16,256,128]{2,1,0:T(8,128)(2,1)} %stack.2), calls=%async_computation | async-start | bytes 2097152 | tf_op jit(solution)/shard_map/all_to_all | solution.py:14
  20.9 1.1 copy.37
  22.3 34.1 %all-gather.3.cloned.1.call-done = bf16[4096,128]{1,0:T(8,128)(2,1)} async-done(((bf16[256,128]{1,0:T(8,128)(2,1)}), bf16[4096,128]{1,0:T(8,128)(2,1)}) %all-gather.3.cloned.1.call-update) | async-done | bytes 1048592 | tf_op jit(solution)/shard_map/all_gather | solution.py:81
  56.4 24.5 %while.35 = (s32[]{:T(128)}, f32[1,4,256]{2,1,0:T(4,128)S(1)}, f32[1,4,256]{2,1,0:T(4,128)S(1)}, f32[1,4,256,128]{3,2,1,0:T(8,128)S(1)}, s32[32]{0:T(128)S(1)}, ...) while((s32[]{:T(128)}, f32[1,4,256]{2,1,0:T(4,128)S(1)}, ...), condition=%wide.region_3.6_spmd.clone, body=%wide.region_0.5_spmd.clone.sunk | while | flops 551443584 | bytes 16618426 | solution.py:93
  60.0 2.4 %fusion.103 = f32[1,4,256,128]{3,2,1,0:T(8,128)S(1)} fusion(f32[1024,256,4]{1,0,2:T(8,128)S(1)} %get-tuple-element.745, f32[4,256]{1,0:T(4,128)S(1)} %bitcast.247, pred[256,1024]{0,1:T(8,128)(4,1)S(1)} %copy.70, f32[1,4,256,128]{3,2,1,0:T(8,128)S(1)} %get-tuple-element.783, bf16[4096,128]{1,0:T(8,128)(2,1)} %get-tuple-element.807, ...), kind=kOutput, calls=%fused_computation.12.clone.1 | convolution fusion | flops 274071552 | bytes 5775365 | tf_op jit(solution)/shard_map/while/body/eval_jaxpr/ghqk,kgd->ghqd/dot_general | solution.py:66
  65.1 1.0 fusion.102
  66.1 2.4 %fusion.103 = f32[1,4,256,128]{3,2,1,0:T(8,128)S(1)} fusion(f32[1024,256,4]{1,0,2:T(8,128)S(1)} %get-tuple-element.745, f32[4,256]{1,0:T(4,128)S(1)} %bitcast.247, pred[256,1024]{0,1:T(8,128)(4,1)S(1)} %copy.70, f32[1,4,256,128]{3,2,1,0:T(8,128)S(1)} %get-tuple-element.783, bf16[4096,128]{1,0:T(8,128)(2,1)} %get-tuple-element.807, ...), kind=kOutput, calls=%fused_computation.12.clone.1 | convolution fusion | flops 274071552 | bytes 5775365 | tf_op jit(solution)/shard_map/while/body/eval_jaxpr/ghqk,kgd->ghqd/dot_general | solution.py:66
  71.2 1.0 fusion.102
  72.3 2.4 %fusion.103 = f32[1,4,256,128]{3,2,1,0:T(8,128)S(1)} fusion(f32[1024,256,4]{1,0,2:T(8,128)S(1)} %get-tuple-element.745, f32[4,256]{1,0:T(4,128)S(1)} %bitcast.247, pred[256,1024]{0,1:T(8,128)(4,1)S(1)} %copy.70, f32[1,4,256,128]{3,2,1,0:T(8,128)S(1)} %get-tuple-element.783, bf16[4096,128]{1,0:T(8,128)(2,1)} %get-tuple-element.807, ...), kind=kOutput, calls=%fused_computation.12.clone.1 | convolution fusion | flops 274071552 | bytes 5775365 | tf_op jit(solution)/shard_map/while/body/eval_jaxpr/ghqk,kgd->ghqd/dot_general | solution.py:66
  78.4 2.4 %fusion.103 = f32[1,4,256,128]{3,2,1,0:T(8,128)S(1)} fusion(f32[1024,256,4]{1,0,2:T(8,128)S(1)} %get-tuple-element.745, f32[4,256]{1,0:T(4,128)S(1)} %bitcast.247, pred[256,1024]{0,1:T(8,128)(4,1)S(1)} %copy.70, f32[1,4,256,128]{3,2,1,0:T(8,128)S(1)} %get-tuple-element.783, bf16[4096,128]{1,0:T(8,128)(2,1)} %get-tuple-element.807, ...), kind=kOutput, calls=%fused_computation.12.clone.1 | convolution fusion | flops 274071552 | bytes 5775365 | tf_op jit(solution)/shard_map/while/body/eval_jaxpr/ghqk,kgd->ghqd/dot_general | solution.py:66
  81.2 15.1 %all-gather.5.cloned.1.call-done = bf16[4096,128]{1,0:T(8,128)(2,1)} async-done(((bf16[256,128]{1,0:T(8,128)(2,1)}), bf16[4096,128]{1,0:T(8,128)(2,1)}) %all-gather.5.cloned.1.call-update) | async-done | bytes 1048592 | tf_op jit(solution)/shard_map/all_gather | solution.py:133
  96.3 47.3 %while.36 = (s32[]{:T(128)}, f32[256,1,4,128]{0,3,2,1:T(8,128)S(1)}, bf16[4,1024,256]{1,2,0:T(8,128)(2,1)}, s32[4]{0:T(128)S(1)}, bf16[4096,128]{1,0:T(8,128)(2,...) while((s32[]{:T(128)}, ...), condition=%wide.region_6.9_spmd.clone, body=%wide.region_5.8_spmd.clone.sunk | while | flops 1357005952 | bytes 25215972 | solution.py:150
  99.3 1.7 fusion.114
  100.9 1.5 fusion.117
  102.5 2.5 %fusion.115 = bf16[1,4,256,1024]{2,3,1,0:T(8,128)(2,1)S(1)} fusion(f32[1024,256,4]{1,0,2:T(8,128)S(1)} %fusion.114, f32[4,256]{1,0:T(4,128)S(1)} %bitcast.253, f32[4,256]{1,0:T(4,128)S(1)} %bitcast.255, pred[256,1024]{0,1:T(8,128)(4,1)S(1)} %copy.73, bf16[256,1,4,128]{0,3,2,1:T(8,128)(2,1)S(1)} %get-tuple-element.869, ...), kind=kOutput, calls=%fused_computation.40.clone.1 | convolution fusion | flops 275775488 | bytes 7086084 | tf_op jit(solution)/shard_map/while/body/eval_jaxpr/qghd,kgd->ghqk/dot_general | solution.py:110
  105.8 1.5 fusion.116
  111.1 1.6 fusion.114
  112.8 1.5 fusion.117
  114.3 2.5 %fusion.115 = bf16[1,4,256,1024]{2,3,1,0:T(8,128)(2,1)S(1)} fusion(f32[1024,256,4]{1,0,2:T(8,128)S(1)} %fusion.114, f32[4,256]{1,0:T(4,128)S(1)} %bitcast.253, f32[4,256]{1,0:T(4,128)S(1)} %bitcast.255, pred[256,1024]{0,1:T(8,128)(4,1)S(1)} %copy.73, bf16[256,1,4,128]{0,3,2,1:T(8,128)(2,1)S(1)} %get-tuple-element.869, ...), kind=kOutput, calls=%fused_computation.40.clone.1 | convolution fusion | flops 275775488 | bytes 7086084 | tf_op jit(solution)/shard_map/while/body/eval_jaxpr/qghd,kgd->ghqk/dot_general | solution.py:110
  117.6 1.5 fusion.116
  122.9 1.6 fusion.114
  124.6 1.5 fusion.117
  126.1 2.5 %fusion.115 = bf16[1,4,256,1024]{2,3,1,0:T(8,128)(2,1)S(1)} fusion(f32[1024,256,4]{1,0,2:T(8,128)S(1)} %fusion.114, f32[4,256]{1,0:T(4,128)S(1)} %bitcast.253, f32[4,256]{1,0:T(4,128)S(1)} %bitcast.255, pred[256,1024]{0,1:T(8,128)(4,1)S(1)} %copy.73, bf16[256,1,4,128]{0,3,2,1:T(8,128)(2,1)S(1)} %get-tuple-element.869, ...), kind=kOutput, calls=%fused_computation.40.clone.1 | convolution fusion | flops 275775488 | bytes 7086084 | tf_op jit(solution)/shard_map/while/body/eval_jaxpr/qghd,kgd->ghqk/dot_general | solution.py:110
  129.4 1.5 fusion.116
  134.8 1.7 fusion.114
  136.4 1.5 fusion.117
  138.0 2.5 %fusion.115 = bf16[1,4,256,1024]{2,3,1,0:T(8,128)(2,1)S(1)} fusion(f32[1024,256,4]{1,0,2:T(8,128)S(1)} %fusion.114, f32[4,256]{1,0:T(4,128)S(1)} %bitcast.253, f32[4,256]{1,0:T(4,128)S(1)} %bitcast.255, pred[256,1024]{0,1:T(8,128)(4,1)S(1)} %copy.73, bf16[256,1,4,128]{0,3,2,1:T(8,128)(2,1)S(1)} %get-tuple-element.869, ...), kind=kOutput, calls=%fused_computation.40.clone.1 | convolution fusion | flops 275775488 | bytes 7086084 | tf_op jit(solution)/shard_map/while/body/eval_jaxpr/qghd,kgd->ghqk/dot_general | solution.py:110
  141.2 1.5 fusion.116
  143.6 3.9 %copy.45 = bf16[4,1024,256]{2,1,0:T(8,128)(2,1)} copy(bf16[4,1024,256]{1,2,0:T(8,128)(2,1)} %get-tuple-element.424) | data formatting | bytes 4194304 | tf_op jit(solution)/shard_map/convert_element_type | solution.py:160
  149.4 57.0 %reduce-scatter.2.cloned.1.call-done = bf16[256,256]{1,0:T(8,128)(2,1)} async-done(((bf16[4096,256]{1,0:T(8,128)(2,1)}), bf16[256,256]{1,0:T(8,128)(2,1)}) %reduce-scatter.2.cloned.1.call-update) | async-done | bytes 131088 | tf_op jit(solution)/shard_map/reduce_scatter | solution.py:159
  206.4 1.6 fusion.75
  (150 shorter events, 33.6 us)
Async XLA Ops:
  7.2 13.0 %copy-start = (s32[32,32]{1,0:T(8,128)S(1)}, s32[32,32]{1,0:T(8,128)}, u32[]{:S(2)}) copy-start(s32[32,32]{1,0:T(8,128)} %param.19) | copy-start | bytes 12292
  7.2 49.2 %copy-start.2 = (s32[32]{0:T(128)S(1)}, s32[32]{0:T(128)}, u32[]{:S(2)}) copy-start(s32[32]{0:T(128)} %param.18) | copy-start | bytes 388
  7.2 14.9 %copy-start.1 = (bf16[256,512]{1,0:T(8,128)(2,1)S(1)}, bf16[256,512]{1,0:T(8,128)(2,1)}, u32[]{:S(2)}) copy-start(bf16[256,512]{1,0:T(8,128)(2,1)} %param.17) | copy-start | bytes 786436
  7.2 49.2 %all-gather.3.cloned.1.call-start = ((), (), s32[]{:S(2)}) async-start(), calls=%async_computation.2 | async-start | bytes 1114112 | tf_op jit(solution)/shard_map/all_gather | solution.py:81
  10.0 46.4 %all-to-all-start = ((bf16[16,256,128]{2,1,0:T(8,128)(2,1)}), bf16[16,256,128]{2,1,0:T(8,128)(2,1)S(1)}, u32[]{:S(2)}, u32[]{:S(2)}) async-start(bf16[16,256,128]{2,1,0:T(8,128)(2,1)} %stack.2), calls=%async_computation | async-start | bytes 2097152 | tf_op jit(solution)/shard_map/all_to_all | solution.py:14
  18.5 77.7 %all-gather.5.cloned.1.call-start = ((), (), s32[]{:S(2)}) async-start(), calls=%async_computation.3 | async-start | bytes 1114112 | tf_op jit(solution)/shard_map/all_gather | solution.py:133
  19.3 187.1 %reduce-scatter.2.cloned.1.call-start = ((), (), s32[]{:S(2)}) async-start(), calls=%async_computation.4 | async-start | bytes 2228224 | tf_op jit(solution)/shard_map/reduce_scatter | solution.py:159
Sparse Core Ops, SparseCore 0:
  9.8 46.4 all-gather.2
  58.2 38.0 all-gather.4
  147.7 58.6 reduce-scatter.1
